TPU v7x, 128 devices: a whole 4x4x4 slice. The times are simulated.
128 devices in a mesh: section: 8 (over y_hi, z), seq: 16 (over x, y_lo, core).
Axes of the slice: x: 4, y: 4 (y_hi: 2, y_lo: 2; y = y_hi * 2 + y_lo), z: 4, core: 2. Of those that a mesh axis runs over, the one named last changes fastest.
Arguments:
- inbound_embedding_batches: bfloat16 [2, 128, 4096], replicated, may hold values from -16 to 16
- decoder_embedding_batches: bfloat16 [2, 128, 4096], replicated, may hold values from -16 to 16
- asking_projections: bfloat16 [8, 4096, 4096], P('section', None, 'seq'), may hold values from -0.09375 to 0.09375
- probe_projections: bfloat16 [8, 4096, 4096], P('section', None, 'seq'), may hold values from -0.09375 to 0.09375
- payload_projections: bfloat16 [8, 4096, 4096], P('section', None, 'seq'), may hold values from -0.09375 to 0.09375
- exit_projections: bfloat16 [8, 4096, 4096], P('section', 'seq'), may hold values from -0.1875 to 0.1875
- layer_rescale_weights: float32 [8, 4096], P('section'), may hold values from 0.1 to 1.9
- logit_sharpness: float32 [8, 64], P('section', 'seq'), may hold values from 0.5 to 3
- last_rescale_weights: float32 [4096], replicated, may hold values from 0.1 to 1.9
Outputs:
- section_out: bfloat16 [8, 2, 128, 4096], P('section')
All inputs are finite; a program needn't handle non-finite values.
Results may differ from a plain program's by a relative error of at most 0.025.
Values may be sent and summed in bfloat16 or wider, within the bound.
A program may use at most 64 MiB of HBM per device.

v0:
```python
import math
import jax
import jax.numpy as jnp
from jax import lax
from jax.sharding import PartitionSpec as P

epsilon = 1e-06


def from_behind(x, axis, by):
    count = lax.axis_size(axis)
    pairs = [(i, i + by) for i in range(count) if 0 <= i + by < count]
    return lax.ppermute(x, axis, pairs)


def broadcast(value, axis, source):
    kept = jnp.where(lax.axis_index(axis) == source, value, 0).astype(value.dtype)
    return lax.psum(kept, axis)


def normalize(row_block, gain_vector):
    values = row_block.astype(jnp.float32)
    factor = lax.rsqrt(jnp.mean(values * values, axis=-1, keepdims=True) + epsilon)
    return (values * factor * gain_vector).astype(jnp.bfloat16)


def unit_heads(projected):
    return (
        projected * lax.rsqrt(jnp.mean(projected * projected, axis=-1, keepdims=True) + epsilon)
    ).astype(jnp.bfloat16)


def attend(queries, keys_proj, values_proj, logit_divisor):
    length = queries.shape[0]
    key_length = keys_proj.shape[0]
    head_count = logit_divisor.shape[0]
    head_size = queries.shape[1] // head_count
    unit_query = unit_heads(queries.reshape(length, head_count, head_size))
    unit_key = unit_heads(keys_proj.reshape(key_length, head_count, head_size))
    values = values_proj.astype(jnp.bfloat16).reshape(key_length, head_count, head_size)
    scores = jnp.einsum("qhd,khd->hqk", unit_query, unit_key, preferred_element_type=jnp.float32)
    scores = scores * (logit_divisor[:, None, None] / math.sqrt(head_size))
    weights = jnp.exp(scores)
    weights = (weights / jnp.sum(weights, axis=-1, keepdims=True)).astype(jnp.bfloat16)
    blended_payloads = jnp.einsum(
        "hqk,khd->qhd", weights, values, preferred_element_type=jnp.float32
    )
    return blended_payloads.astype(jnp.bfloat16).reshape(length, head_count * head_size)


def shards(
    inbound_embedding_batches,
    decoder_embedding_batches,
    asking_projections,
    probe_projections,
    payload_projections,
    exit_projections,
    layer_rescale_weights,
    logit_sharpness,
    last_rescale_weights,
):
    section_count = lax.axis_size("section")
    seq_count = lax.axis_size("seq")
    present_layer_index = lax.axis_index("section")
    seq_index = lax.axis_index("seq")
    encoders = 3 * section_count // 8
    batches = inbound_embedding_batches.shape[0]
    length = inbound_embedding_batches.shape[1]
    width = inbound_embedding_batches.shape[2]
    share_rows = length // seq_count
    first_own = seq_index * share_rows
    ticks = section_count + batches - 1
    w_query = asking_projections[0]
    w_key = probe_projections[0]
    w_value = payload_projections[0]
    w_output = exit_projections[0]
    logit_divisor = logit_sharpness[0]
    gain_vector = layer_rescale_weights[0]
    is_encoder = present_layer_index < encoders

    def layer(stream, memory_raw):
        rescaled_activations = normalize(stream, gain_vector)
        remote = normalize(memory_raw, last_rescale_weights)
        source_kv = jnp.where(is_encoder, rescaled_activations, remote)
        queries = jnp.dot(rescaled_activations, w_query, preferred_element_type=jnp.float32)
        keys_proj = jnp.dot(source_kv, w_key, preferred_element_type=jnp.float32)
        values_proj = jnp.dot(source_kv, w_value, preferred_element_type=jnp.float32)
        blended_payloads = attend(queries, keys_proj, values_proj, logit_divisor)
        update = lax.psum_scatter(
            jnp.dot(blended_payloads, w_output, preferred_element_type=jnp.float32).astype(
                jnp.bfloat16
            ),
            "seq",
            scatter_dimension=0,
            tiled=True,
        ).astype(jnp.float32)
        own_rows = lax.dynamic_slice_in_dim(stream, first_own, share_rows, 0)
        return (own_rows.astype(jnp.float32) + update).astype(jnp.bfloat16)

    blank = jnp.zeros((length, width), inbound_embedding_batches.dtype)
    holder = jnp.zeros((batches,) + blank.shape, inbound_embedding_batches.dtype)

    def advance(tick_index, state_tuple):
        arrived, carried, stored, finished = state_tuple
        offset = tick_index - present_layer_index
        batch_index = jnp.clip(offset, 0, batches - 1)
        valid = (offset >= 0) & (offset < batches)
        source_rows = lax.dynamic_index_in_dim(
            inbound_embedding_batches, batch_index, 0, keepdims=False
        )
        target_rows = lax.dynamic_index_in_dim(
            decoder_embedding_batches, batch_index, 0, keepdims=False
        )
        memory_kept = lax.dynamic_index_in_dim(stored, batch_index, 0, keepdims=False)
        arrived_rows = arrived
        stream = jnp.where(
            present_layer_index == 0,
            source_rows,
            jnp.where(present_layer_index == encoders, target_rows, arrived_rows),
        )
        share = layer(stream, memory_kept)
        outgoing = lax.all_gather(share, "seq", axis=0, tiled=True)
        written = lax.dynamic_update_index_in_dim(finished, outgoing, batch_index, 0)
        finished = jnp.where(valid, written, finished)
        arrived = from_behind(outgoing, "section", 1)
        encoded = broadcast(outgoing, "section", encoders - 1)
        produced = tick_index - (encoders - 1)
        ready = (produced >= 0) & (produced < batches)
        placed = lax.dynamic_update_index_in_dim(
            stored, encoded, jnp.clip(produced, 0, batches - 1), 0
        )
        stored = jnp.where(ready, placed, stored)
        return (arrived, carried, stored, finished)

    final_state = lax.fori_loop(0, ticks, advance, (blank, blank, holder, holder))
    finished = final_state[3]
    return finished[None]


def solution(mesh):
    return jax.shard_map(
        shards,
        mesh=mesh,
        in_specs=(
            P(),
            P(),
            P("section", None, "seq"),
            P("section", None, "seq"),
            P("section", None, "seq"),
            P("section", "seq", None),
            P("section", None),
            P("section", "seq"),
            P(),
        ),
        out_specs=P("section", None, None, None),
        check_vma=False,
    )
```

profile of v0, /device:TPU:0, one launch (start us, length us, event | category | flops | bytes accessed | tf_op | source)
XLA Modules:
  0.0 1826.0 jit_solution(14866793786622618340)
XLA Ops:
  9.4 1809.7 %while.19 = (s32[]{:T(128)}, bf16[128,4096]{1,0:T(8,128)(2,1)}, bf16[2,128,4096]{2,1,0:T(8,128)(2,1)S(1)}, bf16[2,128,4096]{2,1,0:T(8,128)(2,1)}, pred[]{:T(512)...) while((s32[]{:T(128)}, bf16[128,4096]{1,0:T(8,128)(2,1)}, ...), condition=%wide.region_8.9_spmd, body=%wide.region_0.8_spmd.sunk | while | flops 1104807808 | bytes 77665632 | solution.py:135
  24.5 65.1 %reduce-scatter.2.cloned.1.call-done = bf16[8,4096]{1,0:T(8,128)(2,1)} async-done(((bf16[128,4096]{1,0:T(8,128)(2,1)}), bf16[8,4096]{1,0:T(8,128)(2,1)}) %reduce-scatter.2.cloned.1.call-update) | async-done | bytes 65552 | tf_op jit(solution)/shard_map/while/body/eval_jaxpr/reduce_scatter | solution.py:89
  130.2 83.9 %all-reduce.2.cloned.1.call-done = bf16[1,128,4096]{2,1,0:T(8,128)(2,1)} async-done(((bf16[1,128,4096]{2,1,0:T(8,128)(2,1)}), bf16[1,128,4096]{2,1,0:T(8,128)(2,1)}) %all-reduce.2.cloned.1.call-update) | async-done | bytes 1048592 | tf_op jit(solution)/shard_map/while/body/eval_jaxpr/psum | solution.py:18
  229.5 60.3 %reduce-scatter.2.cloned.1.call-done = bf16[8,4096]{1,0:T(8,128)(2,1)} async-done(((bf16[128,4096]{1,0:T(8,128)(2,1)}), bf16[8,4096]{1,0:T(8,128)(2,1)}) %reduce-scatter.2.cloned.1.call-update) | async-done | bytes 65552 | tf_op jit(solution)/shard_map/while/body/eval_jaxpr/reduce_scatter | solution.py:89
  291.3 30.7 %all-gather.2.cloned.1.call-done = bf16[128,4096]{1,0:T(8,128)(2,1)} async-done(((bf16[8,4096]{1,0:T(8,128)(2,1)}), bf16[128,4096]{1,0:T(8,128)(2,1)}) %all-gather.2.cloned.1.call-update) | async-done | bytes 1048592 | tf_op jit(solution)/shard_map/while/body/eval_jaxpr/all_gather | solution.py:122
  330.5 83.7 %all-reduce.2.cloned.1.call-done = bf16[1,128,4096]{2,1,0:T(8,128)(2,1)} async-done(((bf16[1,128,4096]{2,1,0:T(8,128)(2,1)}), bf16[1,128,4096]{2,1,0:T(8,128)(2,1)}) %all-reduce.2.cloned.1.call-update) | async-done | bytes 1048592 | tf_op jit(solution)/shard_map/while/body/eval_jaxpr/psum | solution.py:18
  429.7 60.4 %reduce-scatter.2.cloned.1.call-done = bf16[8,4096]{1,0:T(8,128)(2,1)} async-done(((bf16[128,4096]{1,0:T(8,128)(2,1)}), bf16[8,4096]{1,0:T(8,128)(2,1)}) %reduce-scatter.2.cloned.1.call-update) | async-done | bytes 65552 | tf_op jit(solution)/shard_map/while/body/eval_jaxpr/reduce_scatter | solution.py:89
  491.6 30.7 %all-gather.2.cloned.1.call-done = bf16[128,4096]{1,0:T(8,128)(2,1)} async-done(((bf16[8,4096]{1,0:T(8,128)(2,1)}), bf16[128,4096]{1,0:T(8,128)(2,1)}) %all-gather.2.cloned.1.call-update) | async-done | bytes 1048592 | tf_op jit(solution)/shard_map/while/body/eval_jaxpr/all_gather | solution.py:122
  530.8 83.8 %all-reduce.2.cloned.1.call-done = bf16[1,128,4096]{2,1,0:T(8,128)(2,1)} async-done(((bf16[1,128,4096]{2,1,0:T(8,128)(2,1)}), bf16[1,128,4096]{2,1,0:T(8,128)(2,1)}) %all-reduce.2.cloned.1.call-update) | async-done | bytes 1048592 | tf_op jit(solution)/shard_map/while/body/eval_jaxpr/psum | solution.py:18
  631.3 60.4 %reduce-scatter.2.cloned.1.call-done = bf16[8,4096]{1,0:T(8,128)(2,1)} async-done(((bf16[128,4096]{1,0:T(8,128)(2,1)}), bf16[8,4096]{1,0:T(8,128)(2,1)}) %reduce-scatter.2.cloned.1.call-update) | async-done | bytes 65552 | tf_op jit(solution)/shard_map/while/body/eval_jaxpr/reduce_scatter | solution.py:89
  693.3 30.8 %all-gather.2.cloned.1.call-done = bf16[128,4096]{1,0:T(8,128)(2,1)} async-done(((bf16[8,4096]{1,0:T(8,128)(2,1)}), bf16[128,4096]{1,0:T(8,128)(2,1)}) %all-gather.2.cloned.1.call-update) | async-done | bytes 1048592 | tf_op jit(solution)/shard_map/while/body/eval_jaxpr/all_gather | solution.py:122
  732.5 83.7 %all-reduce.2.cloned.1.call-done = bf16[1,128,4096]{2,1,0:T(8,128)(2,1)} async-done(((bf16[1,128,4096]{2,1,0:T(8,128)(2,1)}), bf16[1,128,4096]{2,1,0:T(8,128)(2,1)}) %all-reduce.2.cloned.1.call-update) | async-done | bytes 1048592 | tf_op jit(solution)/shard_map/while/body/eval_jaxpr/psum | solution.py:18
  832.9 60.4 %reduce-scatter.2.cloned.1.call-done = bf16[8,4096]{1,0:T(8,128)(2,1)} async-done(((bf16[128,4096]{1,0:T(8,128)(2,1)}), bf16[8,4096]{1,0:T(8,128)(2,1)}) %reduce-scatter.2.cloned.1.call-update) | async-done | bytes 65552 | tf_op jit(solution)/shard_map/while/body/eval_jaxpr/reduce_scatter | solution.py:89
  933.9 83.7 %all-reduce.2.cloned.1.call-done = bf16[1,128,4096]{2,1,0:T(8,128)(2,1)} async-done(((bf16[1,128,4096]{2,1,0:T(8,128)(2,1)}), bf16[1,128,4096]{2,1,0:T(8,128)(2,1)}) %all-reduce.2.cloned.1.call-update) | async-done | bytes 1048592 | tf_op jit(solution)/shard_map/while/body/eval_jaxpr/psum | solution.py:18
  1033.0 60.4 %reduce-scatter.2.cloned.1.call-done = bf16[8,4096]{1,0:T(8,128)(2,1)} async-done(((bf16[128,4096]{1,0:T(8,128)(2,1)}), bf16[8,4096]{1,0:T(8,128)(2,1)}) %reduce-scatter.2.cloned.1.call-update) | async-done | bytes 65552 | tf_op jit(solution)/shard_map/while/body/eval_jaxpr/reduce_scatter | solution.py:89
  1095.0 30.7 %all-gather.2.cloned.1.call-done = bf16[128,4096]{1,0:T(8,128)(2,1)} async-done(((bf16[8,4096]{1,0:T(8,128)(2,1)}), bf16[128,4096]{1,0:T(8,128)(2,1)}) %all-gather.2.cloned.1.call-update) | async-done | bytes 1048592 | tf_op jit(solution)/shard_map/while/body/eval_jaxpr/all_gather | solution.py:122
  1134.1 83.7 %all-reduce.2.cloned.1.call-done = bf16[1,128,4096]{2,1,0:T(8,128)(2,1)} async-done(((bf16[1,128,4096]{2,1,0:T(8,128)(2,1)}), bf16[1,128,4096]{2,1,0:T(8,128)(2,1)}) %all-reduce.2.cloned.1.call-update) | async-done | bytes 1048592 | tf_op jit(solution)/shard_map/while/body/eval_jaxpr/psum | solution.py:18
  1233.3 60.4 %reduce-scatter.2.cloned.1.call-done = bf16[8,4096]{1,0:T(8,128)(2,1)} async-done(((bf16[128,4096]{1,0:T(8,128)(2,1)}), bf16[8,4096]{1,0:T(8,128)(2,1)}) %reduce-scatter.2.cloned.1.call-update) | async-done | bytes 65552 | tf_op jit(solution)/shard_map/while/body/eval_jaxpr/reduce_scatter | solution.py:89
  1334.4 83.8 %all-reduce.2.cloned.1.call-done = bf16[1,128,4096]{2,1,0:T(8,128)(2,1)} async-done(((bf16[1,128,4096]{2,1,0:T(8,128)(2,1)}), bf16[1,128,4096]{2,1,0:T(8,128)(2,1)}) %all-reduce.2.cloned.1.call-update) | async-done | bytes 1048592 | tf_op jit(solution)/shard_map/while/body/eval_jaxpr/psum | solution.py:18
  1433.7 60.3 %reduce-scatter.2.cloned.1.call-done = bf16[8,4096]{1,0:T(8,128)(2,1)} async-done(((bf16[128,4096]{1,0:T(8,128)(2,1)}), bf16[8,4096]{1,0:T(8,128)(2,1)}) %reduce-scatter.2.cloned.1.call-update) | async-done | bytes 65552 | tf_op jit(solution)/shard_map/while/body/eval_jaxpr/reduce_scatter | solution.py:89
  1495.5 30.9 %all-gather.2.cloned.1.call-done = bf16[128,4096]{1,0:T(8,128)(2,1)} async-done(((bf16[8,4096]{1,0:T(8,128)(2,1)}), bf16[128,4096]{1,0:T(8,128)(2,1)}) %all-gather.2.cloned.1.call-update) | async-done | bytes 1048592 | tf_op jit(solution)/shard_map/while/body/eval_jaxpr/all_gather | solution.py:122
  1534.8 83.7 %all-reduce.2.cloned.1.call-done = bf16[1,128,4096]{2,1,0:T(8,128)(2,1)} async-done(((bf16[1,128,4096]{2,1,0:T(8,128)(2,1)}), bf16[1,128,4096]{2,1,0:T(8,128)(2,1)}) %all-reduce.2.cloned.1.call-update) | async-done | bytes 1048592 | tf_op jit(solution)/shard_map/while/body/eval_jaxpr/psum | solution.py:18
  1634.0 60.4 %reduce-scatter.2.cloned.1.call-done = bf16[8,4096]{1,0:T(8,128)(2,1)} async-done(((bf16[128,4096]{1,0:T(8,128)(2,1)}), bf16[8,4096]{1,0:T(8,128)(2,1)}) %reduce-scatter.2.cloned.1.call-update) | async-done | bytes 65552 | tf_op jit(solution)/shard_map/while/body/eval_jaxpr/reduce_scatter | solution.py:89
  1735.1 83.7 %all-reduce.2.cloned.1.call-done = bf16[1,128,4096]{2,1,0:T(8,128)(2,1)} async-done(((bf16[1,128,4096]{2,1,0:T(8,128)(2,1)}), bf16[1,128,4096]{2,1,0:T(8,128)(2,1)}) %all-reduce.2.cloned.1.call-update) | async-done | bytes 1048592 | tf_op jit(solution)/shard_map/while/body/eval_jaxpr/psum | solution.py:18
  (355 shorter events, 355.3 us)
Async XLA Ops:
  24.5 97.2 %all-gather.2.cloned.1.call-start = ((), (), s32[]{:S(2)}) async-start(), calls=%async_computation.2 | async-start | bytes 1114112 | tf_op jit(solution)/shard_map/while/body/eval_jaxpr/all_gather | solution.py:122
  91.1 122.9 %all-reduce.2.cloned.1.call-start = ((), (), s32[]{:S(2)}) async-start(), calls=%async_computation.3 | async-start | bytes 2097152 | tf_op jit(solution)/shard_map/while/body/eval_jaxpr/psum | solution.py:18
  123.3 91.1 %collective-permute-start = (bf16[128,4096]{1,0:T(8,128)(2,1)S(1)}, bf16[128,4096]{1,0:T(8,128)(2,1)}, u32[]{:S(2)}, u32[]{:S(2)}) collective-permute-start(bf16[128,4096]{1,0:T(8,128)(2,1)S(1)} %copy-done), channel_id=1, source_target_pairs={{0,16},{16,32},{32,48},{48,64},{64,80},{80,96},{96,112},{1,17},{17... | collective-permute-start | bytes 3145736 | tf_op jit(solution)/shard_map/while/body/eval_jaxpr/ppermute | solution.py:13
  229.4 92.6 %all-gather.2.cloned.1.call-start = ((), (), s32[]{:S(2)}) async-start(), calls=%async_computation.2 | async-start | bytes 1114112 | tf_op jit(solution)/shard_map/while/body/eval_jaxpr/all_gather | solution.py:122
  291.3 122.9 %all-reduce.2.cloned.1.call-start = ((), (), s32[]{:S(2)}) async-start(), calls=%async_computation.3 | async-start | bytes 2097152 | tf_op jit(solution)/shard_map/while/body/eval_jaxpr/psum | solution.py:18
  323.6 90.9 %collective-permute-start = (bf16[128,4096]{1,0:T(8,128)(2,1)S(1)}, bf16[128,4096]{1,0:T(8,128)(2,1)}, u32[]{:S(2)}, u32[]{:S(2)}) collective-permute-start(bf16[128,4096]{1,0:T(8,128)(2,1)S(1)} %copy-done), channel_id=1, source_target_pairs={{0,16},{16,32},{32,48},{48,64},{64,80},{80,96},{96,112},{1,17},{17... | collective-permute-start | bytes 3145736 | tf_op jit(solution)/shard_map/while/body/eval_jaxpr/ppermute | solution.py:13
  429.6 92.7 %all-gather.2.cloned.1.call-start = ((), (), s32[]{:S(2)}) async-start(), calls=%async_computation.2 | async-start | bytes 1114112 | tf_op jit(solution)/shard_map/while/body/eval_jaxpr/all_gather | solution.py:122
  491.6 123.1 %all-reduce.2.cloned.1.call-start = ((), (), s32[]{:S(2)}) async-start(), calls=%async_computation.3 | async-start | bytes 2097152 | tf_op jit(solution)/shard_map/while/body/eval_jaxpr/psum | solution.py:18
  524.0 92.2 %collective-permute-start = (bf16[128,4096]{1,0:T(8,128)(2,1)S(1)}, bf16[128,4096]{1,0:T(8,128)(2,1)}, u32[]{:S(2)}, u32[]{:S(2)}) collective-permute-start(bf16[128,4096]{1,0:T(8,128)(2,1)S(1)} %copy-done), channel_id=1, source_target_pairs={{0,16},{16,32},{32,48},{48,64},{64,80},{80,96},{96,112},{1,17},{17... | collective-permute-start | bytes 3145736 | tf_op jit(solution)/shard_map/while/body/eval_jaxpr/ppermute | solution.py:13
  631.2 92.8 %all-gather.2.cloned.1.call-start = ((), (), s32[]{:S(2)}) async-start(), calls=%async_computation.2 | async-start | bytes 1114112 | tf_op jit(solution)/shard_map/while/body/eval_jaxpr/all_gather | solution.py:122
  693.2 123.0 %all-reduce.2.cloned.1.call-start = ((), (), s32[]{:S(2)}) async-start(), calls=%async_computation.3 | async-start | bytes 2097152 | tf_op jit(solution)/shard_map/while/body/eval_jaxpr/psum | solution.py:18
  725.7 92.2 %collective-permute-start = (bf16[128,4096]{1,0:T(8,128)(2,1)S(1)}, bf16[128,4096]{1,0:T(8,128)(2,1)}, u32[]{:S(2)}, u32[]{:S(2)}) collective-permute-start(bf16[128,4096]{1,0:T(8,128)(2,1)S(1)} %copy-done), channel_id=1, source_target_pairs={{0,16},{16,32},{32,48},{48,64},{64,80},{80,96},{96,112},{1,17},{17... | collective-permute-start | bytes 3145736 | tf_op jit(solution)/shard_map/while/body/eval_jaxpr/ppermute | solution.py:13
  832.9 92.5 %all-gather.2.cloned.1.call-start = ((), (), s32[]{:S(2)}) async-start(), calls=%async_computation.2 | async-start | bytes 1114112 | tf_op jit(solution)/shard_map/while/body/eval_jaxpr/all_gather | solution.py:122
  894.8 122.8 %all-reduce.2.cloned.1.call-start = ((), (), s32[]{:S(2)}) async-start(), calls=%async_computation.3 | async-start | bytes 2097152 | tf_op jit(solution)/shard_map/while/body/eval_jaxpr/psum | solution.py:18
  1033.0 92.7 %all-gather.2.cloned.1.call-start = ((), (), s32[]{:S(2)}) async-start(), calls=%async_computation.2 | async-start | bytes 1114112 | tf_op jit(solution)/shard_map/while/body/eval_jaxpr/all_gather | solution.py:122
  1094.9 122.9 %all-reduce.2.cloned.1.call-start = ((), (), s32[]{:S(2)}) async-start(), calls=%async_computation.3 | async-start | bytes 2097152 | tf_op jit(solution)/shard_map/while/body/eval_jaxpr/psum | solution.py:18
  1233.3 92.7 %all-gather.2.cloned.1.call-start = ((), (), s32[]{:S(2)}) async-start(), calls=%async_computation.2 | async-start | bytes 1114112 | tf_op jit(solution)/shard_map/while/body/eval_jaxpr/all_gather | solution.py:122
  1295.2 123.0 %all-reduce.2.cloned.1.call-start = ((), (), s32[]{:S(2)}) async-start(), calls=%async_computation.3 | async-start | bytes 2097152 | tf_op jit(solution)/shard_map/while/body/eval_jaxpr/psum | solution.py:18
  1327.6 91.0 %collective-permute-start = (bf16[128,4096]{1,0:T(8,128)(2,1)S(1)}, bf16[128,4096]{1,0:T(8,128)(2,1)}, u32[]{:S(2)}, u32[]{:S(2)}) collective-permute-start(bf16[128,4096]{1,0:T(8,128)(2,1)S(1)} %copy-done), channel_id=1, source_target_pairs={{0,16},{16,32},{32,48},{48,64},{64,80},{80,96},{96,112},{1,17},{17... | collective-permute-start | bytes 3145736 | tf_op jit(solution)/shard_map/while/body/eval_jaxpr/ppermute | solution.py:13
  1433.6 92.8 %all-gather.2.cloned.1.call-start = ((), (), s32[]{:S(2)}) async-start(), calls=%async_computation.2 | async-start | bytes 1114112 | tf_op jit(solution)/shard_map/while/body/eval_jaxpr/all_gather | solution.py:122
  1495.4 123.2 %all-reduce.2.cloned.1.call-start = ((), (), s32[]{:S(2)}) async-start(), calls=%async_computation.3 | async-start | bytes 2097152 | tf_op jit(solution)/shard_map/while/body/eval_jaxpr/psum | solution.py:18
  1528.0 90.9 %collective-permute-start = (bf16[128,4096]{1,0:T(8,128)(2,1)S(1)}, bf16[128,4096]{1,0:T(8,128)(2,1)}, u32[]{:S(2)}, u32[]{:S(2)}) collective-permute-start(bf16[128,4096]{1,0:T(8,128)(2,1)S(1)} %copy-done), channel_id=1, source_target_pairs={{0,16},{16,32},{32,48},{48,64},{64,80},{80,96},{96,112},{1,17},{17... | collective-permute-start | bytes 3145736 | tf_op jit(solution)/shard_map/while/body/eval_jaxpr/ppermute | solution.py:13
  1634.0 92.6 %all-gather.2.cloned.1.call-start = ((), (), s32[]{:S(2)}) async-start(), calls=%async_computation.2 | async-start | bytes 1114112 | tf_op jit(solution)/shard_map/while/body/eval_jaxpr/all_gather | solution.py:122
  1696.0 122.8 %all-reduce.2.cloned.1.call-start = ((), (), s32[]{:S(2)}) async-start(), calls=%async_computation.3 | async-start | bytes 2097152 | tf_op jit(solution)/shard_map/while/body/eval_jaxpr/psum | solution.py:18
  (69 other events, 2550.6 us)
Sparse Core Ops, SparseCore 0:
  24.6 65.0 reduce-scatter.1
  124.2 89.7 all-reduce.1
  229.6 60.1 reduce-scatter.1
  291.4 30.5 all-gather.1
  324.3 89.8 all-reduce.1
  429.7 60.2 reduce-scatter.1
  491.8 30.5 all-gather.1
  524.9 89.7 all-reduce.1
  631.3 60.3 reduce-scatter.1
  693.4 30.5 all-gather.1
  726.4 89.8 all-reduce.1
  833.0 60.2 reduce-scatter.1
  927.8 89.7 all-reduce.1
  1033.1 60.2 reduce-scatter.1
  1095.1 30.5 all-gather.1
  1128.0 89.8 all-reduce.1
  1233.4 60.2 reduce-scatter.1
  1295.4 30.5 all-gather.1
  1328.5 89.7 all-reduce.1
  1433.7 60.1 reduce-scatter.1
  1495.6 30.6 all-gather.1
  1528.7 89.8 all-reduce.1
  1634.1 60.3 reduce-scatter.1
  1728.9 89.7 all-reduce.1
  (3 shorter events, 91.0 us)
where the time goes:
time: 1830 us
  waiting for transfers between devices  1580 us (86%)
  other arithmetic  91.7 us (5%)
  matrix products  74.8 us (4%)
  starting transfers between devices  41 us (2%)
  local copies, waits for them, and re-layouts  25.1 us (1%)
    psum x9, waiting for transfers between devices, broadcast(): return lax.psum(kept, axis)  754 us
    reduce_scatter x9, waiting for transfers between devices, layer(): lax.psum_scatter(jnp.dot(blended_payloads, w_output, preferred_element_ty...  548 us
    all_gather x9, waiting for transfers between devices, advance(): outgoing = lax.all_gather(share, 'seq', axis=0, tiled=True)  276 us
    ppermute x9, starting transfers between devices, from_behind(): return lax.ppermute(x, axis, pairs)  39.8 us
  transfers between devices with their start and end apart: 36, of which 27 were waited for; matrix products, arithmetic and copies ran while one was open for 1% of the time, Pallas kernels for 0%

commit v1 on v0

--- a/solution.py
+++ b/solution.py
@@ -119,7 +119,9 @@
             jnp.where(present_layer_index == encoders, target_rows, arrived_rows),
         )
         share = layer(stream, memory_kept)
-        outgoing = lax.all_gather(share, "seq", axis=0, tiled=True)
+        outgoing = jnp.concatenate(
+            lax.all_to_all(jnp.stack([share] * lax.axis_size("seq")), "seq", 0, 0), axis=0
+        )
         written = lax.dynamic_update_index_in_dim(finished, outgoing, batch_index, 0)
         finished = jnp.where(valid, written, finished)
         arrived = from_behind(outgoing, "section", 1)

time: 1830 us -> 1720 us (0.940)
  waiting for transfers between devices: 1580 us -> 1440 us
  starting transfers between devices: 41 us -> 74.2 us
    all_gather x9 -> x0, waiting for transfers between devices: 276 us -> none  [advance(): outgoing = lax.all_gather(share, 'seq', axis=0, tiled=True)]
    all_to_all x0 -> x9, waiting for transfers between devices: none -> 147 us  [advance(): lax.all_to_all(jnp.stack([share] * lax.axis_size('seq')), 'seq', 0, 0)]
    all_to_all x0 -> x9, starting transfers between devices: none -> 32.9 us  [advance(): lax.all_to_all(jnp.stack([share] * lax.axis_size('seq')), 'seq', 0, 0)]
  transfers between devices with their start and end apart: 36 -> 36, of which waited for: 27 -> 27; matrix products, arithmetic and copies ran while one was open for 1% -> 2% of each run, Pallas kernels for 0% -> 0%
where the time goes in v1:
time: 1720 us
  waiting for transfers between devices  1440 us (84%)
  other arithmetic  85.6 us (5%)
  matrix products  75 us (4%)
  starting transfers between devices  74.2 us (4%)
  local copies, waits for them, and re-layouts  30.6 us (2%)
    psum x9, waiting for transfers between devices, broadcast(): return lax.psum(kept, axis)  740 us
    reduce_scatter x9, waiting for transfers between devices, layer(): lax.psum_scatter(jnp.dot(blended_payloads, w_output, preferred_element_ty...  549 us
    all_to_all x9, waiting for transfers between devices, advance(): lax.all_to_all(jnp.stack([share] * lax.axis_size('seq')), 'seq', 0, 0)  147 us
    ppermute x9, starting transfers between devices, from_behind(): return lax.ppermute(x, axis, pairs)  40.6 us
  transfers between devices with their start and end apart: 36, of which 27 were waited for; matrix products, arithmetic and copies ran while one was open for 2% of the time, Pallas kernels for 0%

profile of v1, /device:TPU:0, one launch (start us, length us, event | category | flops | bytes accessed | tf_op | source)
XLA Modules:
  0.0 1716.1 jit_solution(12866470893001033991)
XLA Ops:
  9.5 1699.7 %while.19 = (s32[]{:T(128)}, bf16[128,4096]{1,0:T(8,128)(2,1)}, bf16[2,128,4096]{2,1,0:T(8,128)(2,1)S(1)}, bf16[2,128,4096]{2,1,0:T(8,128)(2,1)}, pred[]{:T(512)...) while((s32[]{:T(128)}, bf16[128,4096]{1,0:T(8,128)(2,1)}, ...), condition=%wide.region_8.9_spmd, body=%wide.region_0.8_spmd.sunk | while | flops 1104807808 | bytes 74388784 | solution.py:137
  24.4 65.2 %reduce-scatter.2.cloned.1.call-done = bf16[8,4096]{1,0:T(8,128)(2,1)} async-done(((bf16[128,4096]{1,0:T(8,128)(2,1)}), bf16[8,4096]{1,0:T(8,128)(2,1)}) %reduce-scatter.2.cloned.1.call-update) | async-done | bytes 65552 | tf_op jit(solution)/shard_map/while/body/eval_jaxpr/reduce_scatter | solution.py:89
  95.3 16.4 all-to-all-done
  119.6 82.0 %all-reduce.2.cloned.1.call-done = bf16[1,128,4096]{2,1,0:T(8,128)(2,1)} async-done(((bf16[1,128,4096]{2,1,0:T(8,128)(2,1)}), bf16[1,128,4096]{2,1,0:T(8,128)(2,1)}) %all-reduce.2.cloned.1.call-update) | async-done | bytes 1048592 | tf_op jit(solution)/shard_map/while/body/eval_jaxpr/psum | solution.py:18
  216.9 60.5 %reduce-scatter.2.cloned.1.call-done = bf16[8,4096]{1,0:T(8,128)(2,1)} async-done(((bf16[128,4096]{1,0:T(8,128)(2,1)}), bf16[8,4096]{1,0:T(8,128)(2,1)}) %reduce-scatter.2.cloned.1.call-update) | async-done | bytes 65552 | tf_op jit(solution)/shard_map/while/body/eval_jaxpr/reduce_scatter | solution.py:89
  283.1 16.4 all-to-all-done
  307.3 82.4 %all-reduce.2.cloned.1.call-done = bf16[1,128,4096]{2,1,0:T(8,128)(2,1)} async-done(((bf16[1,128,4096]{2,1,0:T(8,128)(2,1)}), bf16[1,128,4096]{2,1,0:T(8,128)(2,1)}) %all-reduce.2.cloned.1.call-update) | async-done | bytes 1048592 | tf_op jit(solution)/shard_map/while/body/eval_jaxpr/psum | solution.py:18
  405.1 60.4 %reduce-scatter.2.cloned.1.call-done = bf16[8,4096]{1,0:T(8,128)(2,1)} async-done(((bf16[128,4096]{1,0:T(8,128)(2,1)}), bf16[8,4096]{1,0:T(8,128)(2,1)}) %reduce-scatter.2.cloned.1.call-update) | async-done | bytes 65552 | tf_op jit(solution)/shard_map/while/body/eval_jaxpr/reduce_scatter | solution.py:89
  495.7 82.2 %all-reduce.2.cloned.1.call-done = bf16[1,128,4096]{2,1,0:T(8,128)(2,1)} async-done(((bf16[1,128,4096]{2,1,0:T(8,128)(2,1)}), bf16[1,128,4096]{2,1,0:T(8,128)(2,1)}) %all-reduce.2.cloned.1.call-update) | async-done | bytes 1048592 | tf_op jit(solution)/shard_map/while/body/eval_jaxpr/psum | solution.py:18
  594.4 60.4 %reduce-scatter.2.cloned.1.call-done = bf16[8,4096]{1,0:T(8,128)(2,1)} async-done(((bf16[128,4096]{1,0:T(8,128)(2,1)}), bf16[8,4096]{1,0:T(8,128)(2,1)}) %reduce-scatter.2.cloned.1.call-update) | async-done | bytes 65552 | tf_op jit(solution)/shard_map/while/body/eval_jaxpr/reduce_scatter | solution.py:89
  685.0 82.0 %all-reduce.2.cloned.1.call-done = bf16[1,128,4096]{2,1,0:T(8,128)(2,1)} async-done(((bf16[1,128,4096]{2,1,0:T(8,128)(2,1)}), bf16[1,128,4096]{2,1,0:T(8,128)(2,1)}) %all-reduce.2.cloned.1.call-update) | async-done | bytes 1048592 | tf_op jit(solution)/shard_map/while/body/eval_jaxpr/psum | solution.py:18
  783.6 60.4 %reduce-scatter.2.cloned.1.call-done = bf16[8,4096]{1,0:T(8,128)(2,1)} async-done(((bf16[128,4096]{1,0:T(8,128)(2,1)}), bf16[8,4096]{1,0:T(8,128)(2,1)}) %reduce-scatter.2.cloned.1.call-update) | async-done | bytes 65552 | tf_op jit(solution)/shard_map/while/body/eval_jaxpr/reduce_scatter | solution.py:89
  849.7 16.4 all-to-all-done
  874.3 82.0 %all-reduce.2.cloned.1.call-done = bf16[1,128,4096]{2,1,0:T(8,128)(2,1)} async-done(((bf16[1,128,4096]{2,1,0:T(8,128)(2,1)}), bf16[1,128,4096]{2,1,0:T(8,128)(2,1)}) %all-reduce.2.cloned.1.call-update) | async-done | bytes 1048592 | tf_op jit(solution)/shard_map/while/body/eval_jaxpr/psum | solution.py:18
  971.6 60.4 %reduce-scatter.2.cloned.1.call-done = bf16[8,4096]{1,0:T(8,128)(2,1)} async-done(((bf16[128,4096]{1,0:T(8,128)(2,1)}), bf16[8,4096]{1,0:T(8,128)(2,1)}) %reduce-scatter.2.cloned.1.call-update) | async-done | bytes 65552 | tf_op jit(solution)/shard_map/while/body/eval_jaxpr/reduce_scatter | solution.py:89
  1037.7 16.4 all-to-all-done
  1062.2 82.2 %all-reduce.2.cloned.1.call-done = bf16[1,128,4096]{2,1,0:T(8,128)(2,1)} async-done(((bf16[1,128,4096]{2,1,0:T(8,128)(2,1)}), bf16[1,128,4096]{2,1,0:T(8,128)(2,1)}) %all-reduce.2.cloned.1.call-update) | async-done | bytes 1048592 | tf_op jit(solution)/shard_map/while/body/eval_jaxpr/psum | solution.py:18
  1159.8 60.4 %reduce-scatter.2.cloned.1.call-done = bf16[8,4096]{1,0:T(8,128)(2,1)} async-done(((bf16[128,4096]{1,0:T(8,128)(2,1)}), bf16[8,4096]{1,0:T(8,128)(2,1)}) %reduce-scatter.2.cloned.1.call-update) | async-done | bytes 65552 | tf_op jit(solution)/shard_map/while/body/eval_jaxpr/reduce_scatter | solution.py:89
  1250.4 82.2 %all-reduce.2.cloned.1.call-done = bf16[1,128,4096]{2,1,0:T(8,128)(2,1)} async-done(((bf16[1,128,4096]{2,1,0:T(8,128)(2,1)}), bf16[1,128,4096]{2,1,0:T(8,128)(2,1)}) %all-reduce.2.cloned.1.call-update) | async-done | bytes 1048592 | tf_op jit(solution)/shard_map/while/body/eval_jaxpr/psum | solution.py:18
  1347.9 60.4 %reduce-scatter.2.cloned.1.call-done = bf16[8,4096]{1,0:T(8,128)(2,1)} async-done(((bf16[128,4096]{1,0:T(8,128)(2,1)}), bf16[8,4096]{1,0:T(8,128)(2,1)}) %reduce-scatter.2.cloned.1.call-update) | async-done | bytes 65552 | tf_op jit(solution)/shard_map/while/body/eval_jaxpr/reduce_scatter | solution.py:89
  1438.4 82.2 %all-reduce.2.cloned.1.call-done = bf16[1,128,4096]{2,1,0:T(8,128)(2,1)} async-done(((bf16[1,128,4096]{2,1,0:T(8,128)(2,1)}), bf16[1,128,4096]{2,1,0:T(8,128)(2,1)}) %all-reduce.2.cloned.1.call-update) | async-done | bytes 1048592 | tf_op jit(solution)/shard_map/while/body/eval_jaxpr/psum | solution.py:18
  1536.0 60.4 %reduce-scatter.2.cloned.1.call-done = bf16[8,4096]{1,0:T(8,128)(2,1)} async-done(((bf16[128,4096]{1,0:T(8,128)(2,1)}), bf16[8,4096]{1,0:T(8,128)(2,1)}) %reduce-scatter.2.cloned.1.call-update) | async-done | bytes 65552 | tf_op jit(solution)/shard_map/while/body/eval_jaxpr/reduce_scatter | solution.py:89
  1602.1 16.4 all-to-all-done
  1626.6 82.2 %all-reduce.2.cloned.1.call-done = bf16[1,128,4096]{2,1,0:T(8,128)(2,1)} async-done(((bf16[1,128,4096]{2,1,0:T(8,128)(2,1)}), bf16[1,128,4096]{2,1,0:T(8,128)(2,1)}) %all-reduce.2.cloned.1.call-update) | async-done | bytes 1048592 | tf_op jit(solution)/shard_map/while/body/eval_jaxpr/psum | solution.py:18
  (337 shorter events, 331.2 us)
Async XLA Ops:
  9.5 80.1 %reduce-scatter.2.cloned.1.call-start = ((), (), s32[]{:S(2)}) async-start(), calls=%async_computation.2 | async-start | bytes 1114112 | tf_op jit(solution)/shard_map/while/body/eval_jaxpr/reduce_scatter | solution.py:89
  95.2 106.4 %all-reduce.2.cloned.1.call-start = ((), (), s32[]{:S(2)}) async-start(), calls=%async_computation.3 | async-start | bytes 2097152 | tf_op jit(solution)/shard_map/while/body/eval_jaxpr/psum | solution.py:18
  112.8 89.1 %collective-permute-start = (bf16[128,4096]{1,0:T(8,128)(2,1)S(1)}, bf16[128,4096]{1,0:T(8,128)(2,1)}, u32[]{:S(2)}, u32[]{:S(2)}) collective-permute-start(bf16[128,4096]{1,0:T(8,128)(2,1)S(1)} %bitcast.89), channel_id=1, source_target_pairs={{0,16},{16,32},{32,48},{48,64},{64,80},{80,96},{96,112},{1,17},{17... | collective-permute-start | bytes 3145736 | tf_op jit(solution)/shard_map/while/body/eval_jaxpr/ppermute | solution.py:13
  202.0 75.5 %reduce-scatter.2.cloned.1.call-start = ((), (), s32[]{:S(2)}) async-start(), calls=%async_computation.2 | async-start | bytes 1114112 | tf_op jit(solution)/shard_map/while/body/eval_jaxpr/reduce_scatter | solution.py:89
  283.0 106.7 %all-reduce.2.cloned.1.call-start = ((), (), s32[]{:S(2)}) async-start(), calls=%async_computation.3 | async-start | bytes 2097152 | tf_op jit(solution)/shard_map/while/body/eval_jaxpr/psum | solution.py:18
  300.6 89.5 %collective-permute-start = (bf16[128,4096]{1,0:T(8,128)(2,1)S(1)}, bf16[128,4096]{1,0:T(8,128)(2,1)}, u32[]{:S(2)}, u32[]{:S(2)}) collective-permute-start(bf16[128,4096]{1,0:T(8,128)(2,1)S(1)} %bitcast.89), channel_id=1, source_target_pairs={{0,16},{16,32},{32,48},{48,64},{64,80},{80,96},{96,112},{1,17},{17... | collective-permute-start | bytes 3145736 | tf_op jit(solution)/shard_map/while/body/eval_jaxpr/ppermute | solution.py:13
  471.1 106.8 %all-reduce.2.cloned.1.call-start = ((), (), s32[]{:S(2)}) async-start(), calls=%async_computation.3 | async-start | bytes 2097152 | tf_op jit(solution)/shard_map/while/body/eval_jaxpr/psum | solution.py:18
  488.6 90.8 %collective-permute-start = (bf16[128,4096]{1,0:T(8,128)(2,1)S(1)}, bf16[128,4096]{1,0:T(8,128)(2,1)}, u32[]{:S(2)}, u32[]{:S(2)}) collective-permute-start(bf16[128,4096]{1,0:T(8,128)(2,1)S(1)} %bitcast.89), channel_id=1, source_target_pairs={{0,16},{16,32},{32,48},{48,64},{64,80},{80,96},{96,112},{1,17},{17... | collective-permute-start | bytes 3145736 | tf_op jit(solution)/shard_map/while/body/eval_jaxpr/ppermute | solution.py:13
  579.5 75.4 %reduce-scatter.2.cloned.1.call-start = ((), (), s32[]{:S(2)}) async-start(), calls=%async_computation.2 | async-start | bytes 1114112 | tf_op jit(solution)/shard_map/while/body/eval_jaxpr/reduce_scatter | solution.py:89
  660.5 106.6 %all-reduce.2.cloned.1.call-start = ((), (), s32[]{:S(2)}) async-start(), calls=%async_computation.3 | async-start | bytes 2097152 | tf_op jit(solution)/shard_map/while/body/eval_jaxpr/psum | solution.py:18
  678.0 90.6 %collective-permute-start = (bf16[128,4096]{1,0:T(8,128)(2,1)S(1)}, bf16[128,4096]{1,0:T(8,128)(2,1)}, u32[]{:S(2)}, u32[]{:S(2)}) collective-permute-start(bf16[128,4096]{1,0:T(8,128)(2,1)S(1)} %bitcast.89), channel_id=1, source_target_pairs={{0,16},{16,32},{32,48},{48,64},{64,80},{80,96},{96,112},{1,17},{17... | collective-permute-start | bytes 3145736 | tf_op jit(solution)/shard_map/while/body/eval_jaxpr/ppermute | solution.py:13
  849.7 106.6 %all-reduce.2.cloned.1.call-start = ((), (), s32[]{:S(2)}) async-start(), calls=%async_computation.3 | async-start | bytes 2097152 | tf_op jit(solution)/shard_map/while/body/eval_jaxpr/psum | solution.py:18
  867.2 89.4 %collective-permute-start = (bf16[128,4096]{1,0:T(8,128)(2,1)S(1)}, bf16[128,4096]{1,0:T(8,128)(2,1)}, u32[]{:S(2)}, u32[]{:S(2)}) collective-permute-start(bf16[128,4096]{1,0:T(8,128)(2,1)S(1)} %bitcast.89), channel_id=1, source_target_pairs={{0,16},{16,32},{32,48},{48,64},{64,80},{80,96},{96,112},{1,17},{17... | collective-permute-start | bytes 3145736 | tf_op jit(solution)/shard_map/while/body/eval_jaxpr/ppermute | solution.py:13
  1037.6 106.8 %all-reduce.2.cloned.1.call-start = ((), (), s32[]{:S(2)}) async-start(), calls=%async_computation.3 | async-start | bytes 2097152 | tf_op jit(solution)/shard_map/while/body/eval_jaxpr/psum | solution.py:18
  1055.2 89.6 %collective-permute-start = (bf16[128,4096]{1,0:T(8,128)(2,1)S(1)}, bf16[128,4096]{1,0:T(8,128)(2,1)}, u32[]{:S(2)}, u32[]{:S(2)}) collective-permute-start(bf16[128,4096]{1,0:T(8,128)(2,1)S(1)} %bitcast.89), channel_id=1, source_target_pairs={{0,16},{16,32},{32,48},{48,64},{64,80},{80,96},{96,112},{1,17},{17... | collective-permute-start | bytes 3145736 | tf_op jit(solution)/shard_map/while/body/eval_jaxpr/ppermute | solution.py:13
  1144.8 75.4 %reduce-scatter.2.cloned.1.call-start = ((), (), s32[]{:S(2)}) async-start(), calls=%async_computation.2 | async-start | bytes 1114112 | tf_op jit(solution)/shard_map/while/body/eval_jaxpr/reduce_scatter | solution.py:89
  1225.8 106.8 %all-reduce.2.cloned.1.call-start = ((), (), s32[]{:S(2)}) async-start(), calls=%async_computation.3 | async-start | bytes 2097152 | tf_op jit(solution)/shard_map/while/body/eval_jaxpr/psum | solution.py:18
  1243.4 89.6 %collective-permute-start = (bf16[128,4096]{1,0:T(8,128)(2,1)S(1)}, bf16[128,4096]{1,0:T(8,128)(2,1)}, u32[]{:S(2)}, u32[]{:S(2)}) collective-permute-start(bf16[128,4096]{1,0:T(8,128)(2,1)S(1)} %bitcast.89), channel_id=1, source_target_pairs={{0,16},{16,32},{32,48},{48,64},{64,80},{80,96},{96,112},{1,17},{17... | collective-permute-start | bytes 3145736 | tf_op jit(solution)/shard_map/while/body/eval_jaxpr/ppermute | solution.py:13
  1333.0 75.4 %reduce-scatter.2.cloned.1.call-start = ((), (), s32[]{:S(2)}) async-start(), calls=%async_computation.2 | async-start | bytes 1114112 | tf_op jit(solution)/shard_map/while/body/eval_jaxpr/reduce_scatter | solution.py:89
  1414.0 106.7 %all-reduce.2.cloned.1.call-start = ((), (), s32[]{:S(2)}) async-start(), calls=%async_computation.3 | async-start | bytes 2097152 | tf_op jit(solution)/shard_map/while/body/eval_jaxpr/psum | solution.py:18
  1431.5 89.4 %collective-permute-start = (bf16[128,4096]{1,0:T(8,128)(2,1)S(1)}, bf16[128,4096]{1,0:T(8,128)(2,1)}, u32[]{:S(2)}, u32[]{:S(2)}) collective-permute-start(bf16[128,4096]{1,0:T(8,128)(2,1)S(1)} %bitcast.89), channel_id=1, source_target_pairs={{0,16},{16,32},{32,48},{48,64},{64,80},{80,96},{96,112},{1,17},{17... | collective-permute-start | bytes 3145736 | tf_op jit(solution)/shard_map/while/body/eval_jaxpr/ppermute | solution.py:13
  1521.0 75.4 %reduce-scatter.2.cloned.1.call-start = ((), (), s32[]{:S(2)}) async-start(), calls=%async_computation.2 | async-start | bytes 1114112 | tf_op jit(solution)/shard_map/while/body/eval_jaxpr/reduce_scatter | solution.py:89
  1602.1 106.8 %all-reduce.2.cloned.1.call-start = ((), (), s32[]{:S(2)}) async-start(), calls=%async_computation.3 | async-start | bytes 2097152 | tf_op jit(solution)/shard_map/while/body/eval_jaxpr/psum | solution.py:18
  1619.6 89.6 %collective-permute-start = (bf16[128,4096]{1,0:T(8,128)(2,1)S(1)}, bf16[128,4096]{1,0:T(8,128)(2,1)}, u32[]{:S(2)}, u32[]{:S(2)}) collective-permute-start(bf16[128,4096]{1,0:T(8,128)(2,1)S(1)} %bitcast.89), channel_id=1, source_target_pairs={{0,16},{16,32},{32,48},{48,64},{64,80},{80,96},{96,112},{1,17},{17... | collective-permute-start | bytes 3145736 | tf_op jit(solution)/shard_map/while/body/eval_jaxpr/ppermute | solution.py:13
  (60 other events, 1957.8 us)
Sparse Core Ops, SparseCore 0:
  24.6 65.0 reduce-scatter.1
  112.9 88.6 all-reduce.1
  217.0 60.3 reduce-scatter.1
  300.7 88.9 all-reduce.1
  405.2 60.2 reduce-scatter.1
  488.7 89.0 all-reduce.1
  594.6 60.2 reduce-scatter.1
  678.1 88.9 all-reduce.1
  783.8 60.2 reduce-scatter.1
  867.3 88.9 all-reduce.1
  971.8 60.1 reduce-scatter.1
  1055.3 89.1 all-reduce.1
  1159.9 60.2 reduce-scatter.1
  1243.5 89.0 all-reduce.1
  1348.0 60.2 reduce-scatter.1
  1431.6 88.9 all-reduce.1
  1536.1 60.2 reduce-scatter.1
  1619.7 89.0 all-reduce.1
